TPU v7x, 32 devices: a whole 2x2x4 slice. The times are simulated.
32 devices in a mesh: seq: 4 (over y, core), head: 8 (over z, x).
Axes of the slice: x: 2, y: 2, z: 4, core: 2. Of those that a mesh axis runs over, the one named last changes fastest.
Arguments:
- inputs: bfloat16 [4096, 3, 2048], P(('seq', 'head')), may hold values from -6 to 6
- attn_gain: float32 [2048], replicated, may hold values from 0.25 to 1.75
- w_query: bfloat16 [2048, 256], P(None, 'head'), may hold values from -0.125 to 0.125
- w_key: bfloat16 [2048, 256], P(None, 'head'), may hold values from -0.125 to 0.125
- w_value: bfloat16 [2048, 2048], P(None, 'head'), may hold values from -0.125 to 0.125
- w_out: bfloat16 [2048, 2048], P('head'), may hold values from -1.5 to 1.5
- out_bias: float32 [2048], replicated, may hold values from -1.5 to 1.5
- mlp_gain: float32 [2048], replicated, may hold values from 0.25 to 1.75
- gate_weight: bfloat16 [2048, 5504], P(None, 'head'), may hold values from -0.125 to 0.125
- up_weight: bfloat16 [2048, 5504], P(None, 'head'), may hold values from -0.125 to 0.125
- down_weight: bfloat16 [5504, 2048], P('head'), may hold values from -0.078125 to 0.078125
- cotangent: bfloat16 [4096, 3, 2048], P(('seq', 'head')), may hold values from -6 to 6
- doc_lengths: int32 [3, 8], replicated, may hold values from 1 to 1536, 4096 in all within a row
Outputs:
- output: bfloat16 [4096, 3, 2048], P(('seq', 'head'))
- input_grad: bfloat16 [4096, 3, 2048], P(('seq', 'head'))
- attn_gain_grad: float32 [2048], P(('seq', 'head'))
- w_query_grad: float32 [2048, 256], P('seq', 'head')
- w_key_grad: float32 [2048, 256], P('seq', 'head')
- w_value_grad: float32 [2048, 2048], P('seq', 'head')
- w_out_grad: float32 [2048, 2048], P('head', 'seq')
- out_bias_grad: float32 [2048], P(('seq', 'head'))
- mlp_gain_grad: float32 [2048], P(('seq', 'head'))
- w_gate_grad: float32 [2048, 5504], P('seq', 'head')
- w_up_grad: float32 [2048, 5504], P('seq', 'head')
- w_down_grad: float32 [5504, 2048], P('head', 'seq')
Inputs may be any that keep to these rules, and one draw needn't show every extreme that they name: `doc_lengths`: in each row the 8 lengths sum to 4096 and the longest is exactly 1536.
All inputs are finite; a program needn't handle non-finite values.
Results may differ from a plain program's by a relative error of at most 0.02.
Values may be sent and summed in bfloat16 or wider, within the bound.
A program may use at most 320 MiB of HBM per device.

v0:
```python
import jax
import jax.numpy as jnp
from jax import lax
from jax.sharding import PartitionSpec as P

FEAT = 16
epsilon = 1e-05
root_half = 0.7071067811865476
exact_precision_flag = lax.Precision.HIGHEST


def entering(array, axis, join, neutral, backward):
    count = lax.axis_size(axis)
    place = lax.axis_index(axis)
    ahead = count - 1 - place if backward else place
    gathered = jax.tree.map(
        lambda a, kind: lax.all_gather(a.astype(kind), axis),
        array,
        (jnp.bfloat16, jnp.bfloat16, jnp.bfloat16),
    )
    state = jax.tree.map(lambda a, e: jnp.zeros_like(a) + jnp.asarray(e, a.dtype), array, neutral)

    def one(step, state):
        source = count - 1 - step if backward else step
        return join(
            state,
            jax.tree.map(
                lambda a, own: lax.dynamic_index_in_dim(a, source, 0, False).astype(own.dtype),
                gathered,
                array,
            ),
        )

    return lax.fori_loop(0, ahead, one, state)


def features(inputs):
    halved = inputs * 0.5
    size_in = inputs.shape[-1]
    squares = (halved[..., :, None] * halved[..., None, :]).reshape(
        inputs.shape[:-1] + (size_in * size_in,)
    ) * root_half
    return jnp.concatenate(
        [jnp.ones(inputs.shape[:-1] + (1,), inputs.dtype), halved, squares], axis=-1
    )


def doc_layout(doc_lengths, group_begin, group_len):
    doc_ends = jnp.cumsum(doc_lengths, axis=-1)
    positions = group_begin + jnp.arange(group_len, dtype=jnp.int32)
    passed = (doc_ends[..., :, None] <= positions).astype(jnp.int32)
    doc_index = jnp.sum(passed, axis=-2)
    doc_begin = jnp.sum(passed * doc_lengths[..., :, None], axis=-2)
    return (doc_index, doc_begin)


def chain_join(earlier, later):
    keep_prev = 1.0 - later[2]
    return (
        later[0] + keep_prev[:, None, None, None] * earlier[0],
        later[1] + keep_prev[:, None, None] * earlier[1],
        jnp.maximum(earlier[2], later[2]),
    )


def rms_scale(values_in):
    return lax.rsqrt(jnp.mean(values_in * values_in, axis=-1, keepdims=True) + epsilon)


def on_device(
    inputs,
    attn_gain,
    w_query,
    w_key,
    w_value,
    w_out,
    out_bias,
    mlp_gain,
    gate_weight,
    up_weight,
    down_weight,
    cotangent,
    doc_lengths,
):
    shard_len = inputs.shape[0]
    batch_rows = inputs.shape[1]
    head_local = w_query.shape[1] // FEAT
    value_dim = w_value.shape[1] // head_local
    group_len = shard_len * lax.axis_size("head")
    group_begin = lax.axis_index("seq") * group_len
    x_float = inputs.astype(jnp.float32)
    scale_one = rms_scale(x_float)
    normed_one = x_float * scale_one
    normed_low = (normed_one * attn_gain).astype(jnp.bfloat16)
    normed_full = lax.all_gather(normed_low, "head", axis=0, tiled=True)
    query_low = (
        jnp.einsum("trd,dc->trc", normed_full, w_query, preferred_element_type=jnp.float32)
        .astype(jnp.bfloat16)
        .reshape(group_len, batch_rows, head_local, FEAT)
    )
    key_low = (
        jnp.einsum("trd,dc->trc", normed_full, w_key, preferred_element_type=jnp.float32)
        .astype(jnp.bfloat16)
        .reshape(group_len, batch_rows, head_local, FEAT)
    )
    value_low = (
        jnp.einsum("trd,dc->trc", normed_full, w_value, preferred_element_type=jnp.float32)
        .astype(jnp.bfloat16)
        .reshape(group_len, batch_rows, head_local, value_dim)
    )
    doc_index, doc_begin = doc_layout(doc_lengths, group_begin, group_len)
    carried = (doc_begin < group_begin).astype(jnp.float32).T
    trailing = (doc_index == doc_index[:, -1:]).astype(jnp.float32).T
    restart = (doc_begin[:, -1] >= group_begin).astype(jnp.float32)
    positions = jnp.arange(group_len, dtype=jnp.int32)
    visible = (
        (positions[None, :] <= positions[:, None])[None]
        & (doc_index[:, :, None] == doc_index[:, None, :])
    )[:, None]
    scores = (
        jnp.einsum("trhf,urhf->rhtu", query_low, key_low, preferred_element_type=jnp.float32) * 0.25
    )
    weights_low = jnp.where(visible, 1.0 + scores + 0.5 * scores * scores, 0.0).astype(jnp.bfloat16)
    query_float = query_low.astype(jnp.float32)
    key_float = key_low.astype(jnp.float32)
    query_feat = features(query_float).astype(jnp.bfloat16)
    key_feat = features(key_float).astype(jnp.bfloat16)
    trail_low = trailing.astype(jnp.bfloat16)[:, :, None, None]
    local_state = jnp.einsum(
        "trhf,trhv->rhfv", key_feat, value_low * trail_low, preferred_element_type=jnp.float32
    )
    local_sum = jnp.sum(key_feat.astype(jnp.float32) * trailing[:, :, None, None], axis=0)
    empty_chain = (jnp.zeros_like(local_state), jnp.zeros_like(local_sum), jnp.zeros_like(restart))
    state_in, sum_in, _ = entering(
        (local_state, local_sum, restart), "seq", chain_join, empty_chain, False
    )
    state_low = state_in.astype(jnp.bfloat16)
    numerator = jnp.einsum(
        "rhtu,urhv->trhv", weights_low, value_low, preferred_element_type=jnp.float32
    )
    numerator = numerator + carried[:, :, None, None] * jnp.einsum(
        "trhf,rhfv->trhv", query_feat, state_low, preferred_element_type=jnp.float32
    )
    query_feat_float = query_feat.astype(jnp.float32)
    denominator = jnp.transpose(jnp.sum(weights_low, axis=-1, dtype=jnp.float32), (2, 0, 1))
    denominator = denominator + carried[:, :, None] * jnp.einsum(
        "trhf,rhf->trh", query_feat_float, sum_in, precision=exact_precision_flag
    )
    attended = (
        (numerator / denominator[..., None])
        .astype(jnp.bfloat16)
        .reshape(group_len, batch_rows, head_local * value_dim)
    )
    row_segment = attended
    attn_branch = lax.psum_scatter(
        jnp.einsum("trc,cd->trd", row_segment, w_out, preferred_element_type=jnp.float32),
        "head",
        scatter_dimension=0,
        tiled=True,
    )
    middle = x_float + attn_branch + out_bias
    scale_two = rms_scale(middle)
    second_normed = middle * scale_two
    normed_two_low = (second_normed * mlp_gain).astype(jnp.bfloat16)

    def projections(row_segment):
        gate_segment = jnp.einsum(
            "czm,my->czy", row_segment, gate_weight, preferred_element_type=jnp.float32
        )
        up_segment = jnp.einsum(
            "czm,my->czy", row_segment, up_weight, preferred_element_type=jnp.float32
        )
        return (gate_segment, up_segment)

    gate_segment, up_segment = projections(
        lax.all_gather(normed_two_low, "head", axis=0, tiled=True)
    )
    hidden_activation = (jax.nn.silu(gate_segment) * up_segment).astype(jnp.bfloat16)
    row_segment = hidden_activation
    perceptron_branch = lax.psum_scatter(
        jnp.einsum(
            "nzh,hi->nzi", row_segment, down_weight, preferred_element_type=jnp.float32
        ).astype(jnp.bfloat16),
        "head",
        scatter_dimension=0,
        tiled=True,
    ).astype(jnp.float32)
    output = (middle + perceptron_branch).astype(jnp.bfloat16)
    second_normed_complete, gradient_complete = (
        lax.all_gather(normed_two_low, "head", axis=0, tiled=True),
        lax.all_gather(cotangent, "head", axis=0, tiled=True),
    )
    gate_projected, up_projected = projections(second_normed_complete)
    down_weight_gradient = jnp.einsum(
        "ebn,eby->ny", hidden_activation, gradient_complete, preferred_element_type=jnp.float32
    )
    hidden_gradient = jnp.einsum(
        "bje,ke->bjk", gradient_complete, down_weight, preferred_element_type=jnp.float32
    )
    sigmoid_gate = jax.nn.sigmoid(gate_projected)
    gate_gradient = (
        hidden_gradient
        * up_projected
        * sigmoid_gate
        * (1.0 + gate_projected * (1.0 - sigmoid_gate))
    ).astype(jnp.bfloat16)
    up_gradient = (hidden_gradient * gate_projected * sigmoid_gate).astype(jnp.bfloat16)
    grad_w_gate = jnp.einsum(
        "ego,egv->ov", second_normed_complete, gate_gradient, preferred_element_type=jnp.float32
    )
    grad_w_up = jnp.einsum(
        "ego,egv->ov", second_normed_complete, up_gradient, preferred_element_type=jnp.float32
    )
    grad_normed_two = lax.psum_scatter(
        (
            jnp.einsum(
                "szq,hq->szh", gate_gradient, gate_weight, preferred_element_type=jnp.float32
            )
            + jnp.einsum("szq,hq->szh", up_gradient, up_weight, preferred_element_type=jnp.float32)
        ).astype(jnp.bfloat16),
        "head",
        scatter_dimension=0,
        tiled=True,
    ).astype(jnp.float32)
    gain_two_part = jnp.sum(grad_normed_two * second_normed, axis=(0, 1))
    grad_scaled_two = grad_normed_two * mlp_gain
    grad_middle = cotangent.astype(jnp.float32) + scale_two * (
        grad_scaled_two
        - second_normed * jnp.mean(grad_scaled_two * second_normed, axis=-1, keepdims=True)
    )
    bias_part = jnp.sum(grad_middle, axis=(0, 1))
    grad_branch = lax.all_gather(grad_middle.astype(jnp.bfloat16), "head", axis=0, tiled=True)
    grad_w_out = jnp.einsum(
        "trc,trd->cd", attended, grad_branch, preferred_element_type=jnp.float32
    )
    grad_attended = jnp.einsum(
        "trd,cd->trc", grad_branch, w_out, preferred_element_type=jnp.float32
    ).reshape(group_len, batch_rows, head_local, value_dim)
    grad_numer = (grad_attended / denominator[..., None]).astype(jnp.bfloat16)
    grad_denom = -jnp.sum(grad_attended * numerator, axis=-1) / (denominator * denominator)
    grad_weights = (
        jnp.einsum("trhv,urhv->rhtu", grad_numer, value_low, preferred_element_type=jnp.float32)
        + jnp.transpose(grad_denom, (1, 2, 0))[..., None]
    )
    grad_scores = jnp.where(visible, grad_weights * (1.0 + scores), 0.0).astype(jnp.bfloat16)
    grad_query = (
        jnp.einsum("rhtu,urhf->trhf", grad_scores, key_low, preferred_element_type=jnp.float32)
        * 0.25
    )
    grad_key = (
        jnp.einsum("rhtu,trhf->urhf", grad_scores, query_low, preferred_element_type=jnp.float32)
        * 0.25
    )
    grad_value = jnp.einsum(
        "rhtu,trhv->urhv", weights_low, grad_numer, preferred_element_type=jnp.float32
    )
    carry_low = carried.astype(jnp.bfloat16)[:, :, None, None]
    grad_state_in = jnp.einsum(
        "trhf,trhv->rhfv", query_feat, grad_numer * carry_low, preferred_element_type=jnp.float32
    )
    grad_sum_in = jnp.einsum(
        "trhf,trh->rhf",
        query_feat_float,
        carried[:, :, None] * grad_denom,
        precision=exact_precision_flag,
    )
    grad_query_feat = carried[:, :, None, None] * (
        jnp.einsum("trhv,rhfv->trhf", grad_numer, state_low, preferred_element_type=jnp.float32)
        + grad_denom[..., None] * sum_in[None]
    )
    empty_grads = (
        jnp.zeros_like(grad_state_in),
        jnp.zeros_like(grad_sum_in),
        jnp.zeros_like(restart),
    )
    grad_state_out, grad_sum_out, _ = entering(
        (grad_state_in, grad_sum_in, restart), "seq", chain_join, empty_grads, True
    )
    grad_state_low = grad_state_out.astype(jnp.bfloat16)
    grad_key_feat = trailing[:, :, None, None] * (
        jnp.einsum("trhv,rhfv->trhf", value_low, grad_state_low, preferred_element_type=jnp.float32)
        + grad_sum_out[None]
    )
    grad_value = grad_value + trailing[:, :, None, None] * jnp.einsum(
        "trhf,rhfv->trhv", key_feat, grad_state_low, preferred_element_type=jnp.float32
    )
    _, query_map_back = jax.vjp(features, query_float)
    _, key_map_back = jax.vjp(features, key_float)
    grad_query = grad_query + query_map_back(grad_query_feat)[0]
    grad_key = grad_key + key_map_back(grad_key_feat)[0]
    grad_query_low = grad_query.astype(jnp.bfloat16).reshape(
        group_len, batch_rows, head_local * FEAT
    )
    grad_key_low = grad_key.astype(jnp.bfloat16).reshape(group_len, batch_rows, head_local * FEAT)
    grad_value_low = grad_value.astype(jnp.bfloat16).reshape(
        group_len, batch_rows, head_local * value_dim
    )
    grad_w_query = jnp.einsum(
        "trd,trc->dc", normed_full, grad_query_low, preferred_element_type=jnp.float32
    )
    grad_w_key = jnp.einsum(
        "trd,trc->dc", normed_full, grad_key_low, preferred_element_type=jnp.float32
    )
    grad_w_value = jnp.einsum(
        "trd,trc->dc", normed_full, grad_value_low, preferred_element_type=jnp.float32
    )
    summed = jnp.einsum("trc,dc->trd", grad_query_low, w_query, preferred_element_type=jnp.float32)
    summed = summed + jnp.einsum(
        "trc,dc->trd", grad_key_low, w_key, preferred_element_type=jnp.float32
    )
    grad_normed_one = lax.psum_scatter(
        (
            summed
            + jnp.einsum("trc,dc->trd", grad_value_low, w_value, preferred_element_type=jnp.float32)
        ).astype(jnp.bfloat16),
        "head",
        scatter_dimension=0,
        tiled=True,
    ).astype(jnp.float32)
    gain_one_part = jnp.sum(grad_normed_one * normed_one, axis=(0, 1))
    grad_scaled_one = grad_normed_one * attn_gain
    input_grad = (
        grad_middle
        + scale_one
        * (
            grad_scaled_one
            - normed_one * jnp.mean(grad_scaled_one * normed_one, axis=-1, keepdims=True)
        )
    ).astype(jnp.bfloat16)
    gain_one, bias_grad, gain_two = (
        lax.psum_scatter(gain_one_part, ("seq", "head"), scatter_dimension=0, tiled=True),
        lax.psum_scatter(bias_part, ("seq", "head"), scatter_dimension=0, tiled=True),
        lax.psum_scatter(gain_two_part, ("seq", "head"), scatter_dimension=0, tiled=True),
    )
    summed_query, summed_key, summed_value, summed_out, summed_gate, summed_up, summed_down = (
        lax.psum_scatter(
            grad_w_query.astype(jnp.bfloat16), "seq", scatter_dimension=0, tiled=True
        ).astype(jnp.float32),
        lax.psum_scatter(
            grad_w_key.astype(jnp.bfloat16), "seq", scatter_dimension=0, tiled=True
        ).astype(jnp.float32),
        lax.psum_scatter(
            grad_w_value.astype(jnp.bfloat16), "seq", scatter_dimension=0, tiled=True
        ).astype(jnp.float32),
        lax.psum_scatter(
            grad_w_out.astype(jnp.bfloat16), "seq", scatter_dimension=1, tiled=True
        ).astype(jnp.float32),
        lax.psum_scatter(
            grad_w_gate.astype(jnp.bfloat16), "seq", scatter_dimension=0, tiled=True
        ).astype(jnp.float32),
        lax.psum_scatter(
            grad_w_up.astype(jnp.bfloat16), "seq", scatter_dimension=0, tiled=True
        ).astype(jnp.float32),
        lax.psum_scatter(
            down_weight_gradient.astype(jnp.bfloat16), "seq", scatter_dimension=1, tiled=True
        ).astype(jnp.float32),
    )
    return (
        output,
        input_grad,
        gain_one,
        summed_query,
        summed_key,
        summed_value,
        summed_out,
        bias_grad,
        gain_two,
        summed_gate,
        summed_up,
        summed_down,
    )


def solution(mesh):
    placed = (
        P(("seq", "head"), None, None),
        P(),
        P(None, "head"),
        P(None, "head"),
        P(None, "head"),
        P("head", None),
        P(),
        P(),
        P(None, "head"),
        P(None, "head"),
        P("head", None),
        P(("seq", "head"), None, None),
        P(),
    )
    return jax.shard_map(
        on_device,
        mesh=mesh,
        in_specs=placed,
        out_specs=(
            P(("seq", "head"), None, None),
            P(("seq", "head"), None, None),
            P(("seq", "head")),
            P("seq", "head"),
            P("seq", "head"),
            P("seq", "head"),
            P("head", "seq"),
            P(("seq", "head")),
            P(("seq", "head")),
            P("seq", "head"),
            P("seq", "head"),
            P("head", "seq"),
        ),
        check_vma=False,
    )
```

profile of v0, /device:TPU:0, one launch (start us, length us, event | category | flops | bytes accessed | tf_op | source)
XLA Modules:
  0.0 2234.3 jit_solution(17653696838373602096)
XLA Ops:
  14.8 8.3 all-reduce
  28.0 164.0 %all-gather.12.cloned.1.call-done = bf16[1024,3,2048]{2,0,1:T(8,128)(2,1)} async-done(((bf16[128,3,2048]{2,0,1:T(8,128)(2,1)}), bf16[1024,3,2048]{2,0,1:T(8,128)(2,1)}) %all-gather.12.cloned.1.call-update) | async-done | bytes 12582928 | tf_op jit(solution)/shard_map/all_gather | solution.py:95
  192.1 8.6 convolution_convert_fusion.3
  206.8 14.2 convolution_convert_fusion.1
  224.8 4.0 fusion.47
  230.0 3.9 multiply_reduce_fusion
  233.9 5.2 all-gather.2
  241.7 15.4 convert_reduce_fusion
  257.1 8.1 fusion.97
  267.1 4.5 fusion.90
  271.6 4.6 divide_convert_fusion.1
  277.5 10.1 fusion.61
  287.7 412.3 %reduce-scatter.12.cloned.1.call-done = f32[128,3,2048]{2,0,1:T(8,128)} async-done(((f32[1024,3,2048]{2,0,1:T(8,128)}), f32[128,3,2048]{2,0,1:T(8,128)}) %reduce-scatter.12.cloned.1.call-update) | async-done | bytes 3145744 | tf_op jit(solution)/shard_map/reduce_scatter | solution.py:155
  707.0 174.9 %all-gather.14.cloned.1.call-done = bf16[1024,3,2048]{2,0,1:T(8,128)(2,1)} async-done(((bf16[128,3,2048]{2,0,1:T(8,128)(2,1)}), bf16[1024,3,2048]{2,0,1:T(8,128)(2,1)}) %all-gather.14.cloned.1.call-update) | async-done | bytes 12582928 | tf_op jit(solution)/shard_map/all_gather | solution.py:176
  881.9 15.0 fusion.33
  896.8 11.2 fusion.37
  908.1 150.5 %all-gather.16.cloned.1.call-done = bf16[1024,3,2048]{2,0,1:T(8,128)(2,1)} async-done(((bf16[128,3,2048]{2,0,1:T(8,128)(2,1)}), bf16[1024,3,2048]{2,0,1:T(8,128)(2,1)}) %all-gather.16.cloned.1.call-update) | async-done | bytes 12582928 | tf_op jit(solution)/shard_map/all_gather | solution.py:191
  1058.5 22.0 multiply_convert_fusion
  1080.6 17.3 fusion.35
  1097.9 18.9 add_convert_fusion.1
  1116.9 15.2 convolution_convert_fusion
  1132.2 190.8 %reduce-scatter.16.cloned.1.call-done = bf16[128,3,2048]{2,0,1:T(8,128)(2,1)} async-done(((bf16[1024,3,2048]{2,0,1:T(8,128)(2,1)}), bf16[128,3,2048]{2,0,1:T(8,128)(2,1)}) %reduce-scatter.16.cloned.1.call-update) | async-done | bytes 1572880 | tf_op jit(solution)/shard_map/reduce_scatter | solution.py:214
  1323.0 4.0 fusion.20
  1327.0 206.5 %reduce-scatter.14.cloned.1.call-done = bf16[128,3,2048]{2,0,1:T(8,128)(2,1)} async-done(((bf16[1024,3,2048]{2,0,1:T(8,128)(2,1)}), bf16[128,3,2048]{2,0,1:T(8,128)(2,1)}) %reduce-scatter.14.cloned.1.call-update) | async-done | bytes 1572880 | tf_op jit(solution)/shard_map/reduce_scatter | solution.py:180
  1533.4 6.0 fusion.93
  1542.5 175.6 %all-gather.18.cloned.1.call-done = bf16[1024,3,2048]{2,0,1:T(8,128)(2,1)} async-done(((bf16[128,3,2048]{2,0,1:T(8,128)(2,1)}), bf16[1024,3,2048]{2,0,1:T(8,128)(2,1)}) %all-gather.18.cloned.1.call-update) | async-done | bytes 12582928 | tf_op jit(solution)/shard_map/all_gather | solution.py:232
  1718.2 9.0 multiply_reduce_fusion.5
  1732.1 14.5 bitcast_convert_fusion
  1746.7 14.4 bitcast_convert_fusion.1
  1761.1 14.6 bitcast_convert_fusion.2
  1783.6 17.5 select_convert_fusion
  1801.1 6.5 fusion.57
  1810.6 10.3 fusion.78
  1820.9 10.6 fusion.98
  1831.7 9.9 fusion.40
  1841.6 4.9 fusion.88
  1846.5 5.2 all-gather.4
  1851.9 4.9 while.31
  1856.8 5.8 fusion.27
  1870.5 8.2 fusion.58
  1881.7 10.4 fusion.63
  1892.3 7.7 fusion.39
  1900.1 22.1 add_convert_fusion
  1932.7 5.6 reduce-scatter.22.cloned.1.call-done
  1939.7 26.5 %reduce-scatter.24.cloned.1.call-done = bf16[512,256]{1,0:T(8,128)(2,1)} async-done(((bf16[2048,256]{1,0:T(8,128)(2,1)}), bf16[512,256]{1,0:T(8,128)(2,1)}) %reduce-scatter.24.cloned.1.call-update) | async-done | bytes 262160 | tf_op jit(solution)/shard_map/reduce_scatter | solution.py:342
  1968.0 209.8 %reduce-scatter.18.cloned.1.call-done = bf16[128,3,2048]{2,0,1:T(8,128)(2,1)} async-done(((bf16[1024,3,2048]{2,0,1:T(8,128)(2,1)}), bf16[128,3,2048]{2,0,1:T(8,128)(2,1)}) %reduce-scatter.18.cloned.1.call-update) | async-done | bytes 1572880 | tf_op jit(solution)/shard_map/reduce_scatter | solution.py:311
  2181.0 39.7 %all-reduce.4 = (f32[2048]{0:T(1024)S(1)}, f32[2048]{0:T(1024)S(1)}, f32[2048]{0:T(1024)S(1)}) all-reduce(f32[2048]{0:T(1024)S(1)} %get-tuple-element.232, f32[2048]{0:T(1024)S(1)} %copy-done.57, f32[2048]{0:T(1024)S(1)} %copy-done.56), channel_id=11, replica_groups=mesh['seq'=4,'head'=8] {'seq','head'}, use_global_device_ids=true, to_apply=%region_23.24.clone | all-reduce | flops 6144 | bytes 49152
  2222.4 4.9 fusion.16
  (268 shorter events, 89.2 us)
Async XLA Ops:
  7.2 1051.4 %copy-start = (bf16[688,2048]{1,0:T(8,128)(2,1)S(1)}, bf16[688,2048]{1,0:T(8,128)(2,1)}, u32[]{:S(2)}) copy-start(bf16[688,2048]{1,0:T(8,128)(2,1)} %param.27) | copy-start | bytes 8454148
  7.2 184.8 %all-gather.12.cloned.1.call-start = ((), (), s32[]{:S(2)}) async-start(), calls=%async_computation.11 | async-start | bytes 14155776 | tf_op jit(solution)/shard_map/all_gather | solution.py:95
  12.7 179.3 %copy-start.38 = (bf16[2048,32]{0,1:T(8,128)(2,1)S(1)}, bf16[2048,32]{0,1:T(8,128)(2,1)}, u32[]{:S(2)}) copy-start(bf16[2048,32]{0,1:T(8,128)(2,1)} %param.19) | copy-start | bytes 393220
  12.8 252.4 %all-gather.20.cloned.1.call-start = ((), (), s32[]{:S(2)}) async-start(), calls=%async_computation.26 | async-start | bytes 2096640 | tf_op jit(solution)/shard_map/all_gather | solution.py:17
  23.3 248.3 %copy-start.63 = (bf16[273]{0:T(512)(128)(2,1)}, bf16[273]{0:T(512)(128)(2,1)S(1)}, u32[]{:S(2)}) copy-start(bf16[273]{0:T(512)(128)(2,1)S(1)} %pad.3.clone) | copy-start | bytes 1642
  24.4 247.2 %copy-start.35 = (f32[3,1024]{1,0:T(4,128)}, f32[3,1024]{1,0:T(4,128)S(1)}, u32[]{:S(2)}) copy-start(f32[3,1024]{1,0:T(4,128)S(1)} %get-tuple-element.276) | copy-start | bytes 36868
  24.5 205.6 %copy-start.44 = (f32[1024,3]{0,1:T(4,128)}, f32[1024,3]{0,1:T(4,128)S(1)}, u32[]{:S(2)}) copy-start(f32[1024,3]{0,1:T(4,128)S(1)} %get-tuple-element.282) | copy-start | bytes 36868
  28.0 173.5 %copy-start.40 = (bf16[2048,32]{0,1:T(8,128)(2,1)S(1)}, bf16[2048,32]{0,1:T(8,128)(2,1)}, u32[]{:S(2)}) copy-start(bf16[2048,32]{0,1:T(8,128)(2,1)} %param.20) | copy-start | bytes 393220
  200.6 41.1 %copy-start.25 = (bf16[1024,3,32]{0,2,1:T(8,128)(2,1)}, bf16[1024,3,32]{0,2,1:T(8,128)(2,1)S(1)}, u32[]{:S(2)}) copy-start(bf16[1024,3,32]{0,2,1:T(8,128)(2,1)S(1)} %convolution_convert_fusion.3) | copy-start | bytes 589828
  206.8 17.1 copy-start.16
  230.0 470.0 %reduce-scatter.12.cloned.1.call-start = ((), (), s32[]{:S(2)}) async-start(), calls=%async_computation.12 | async-start | bytes 28311552 | tf_op jit(solution)/shard_map/reduce_scatter | solution.py:155
  241.7 15.4 copy-start.9
  257.1 14.5 copy-start.50
  287.6 412.4 %copy-start.60 = (f32[2048]{0:T(1024)S(1)}, f32[2048]{0:T(1024)}, u32[]{:S(2)}) copy-start(f32[2048]{0:T(1024)} %param.23) | copy-start | bytes 24580
  287.6 417.1 %copy-start.54 = (f32[2048]{0:T(1024)S(1)}, f32[2048]{0:T(1024)}, u32[]{:S(2)}) copy-start(f32[2048]{0:T(1024)} %param.24) | copy-start | bytes 24580
  287.6 594.2 %all-gather.14.cloned.1.call-start = ((), (), s32[]{:S(2)}) async-start(), calls=%async_computation.13 | async-start | bytes 14155776 | tf_op jit(solution)/shard_map/all_gather | solution.py:176
  706.1 352.4 %all-gather.16.cloned.1.call-start = ((), (), s32[]{:S(2)}) async-start(), calls=%async_computation.15 | async-start | bytes 14155776 | tf_op jit(solution)/shard_map/all_gather | solution.py:191
  706.7 616.2 %reduce-scatter.16.cloned.1.call-start = ((), (), s32[]{:S(2)}) async-start(), calls=%async_computation.16 | async-start | bytes 14155776 | tf_op jit(solution)/shard_map/reduce_scatter | solution.py:214
  881.9 15.0 copy-start.65
  881.9 15.0 copy-start.66
  1116.8 416.6 %reduce-scatter.14.cloned.1.call-start = ((), (), s32[]{:S(2)}) async-start(), calls=%async_computation.14 | async-start | bytes 14155776 | tf_op jit(solution)/shard_map/reduce_scatter | solution.py:180
  1132.1 401.3 %copy-start.20 = (bf16[128,3,2048]{2,0,1:T(8,128)(2,1)S(1)}, bf16[128,3,2048]{2,0,1:T(8,128)(2,1)}, u32[]{:S(2)}) copy-start(bf16[128,3,2048]{2,0,1:T(8,128)(2,1)} %param.28) | copy-start | bytes 4718596
  1132.1 586.0 %all-gather.18.cloned.1.call-start = ((), (), s32[]{:S(2)}) async-start(), calls=%async_computation.17 | async-start | bytes 14155776 | tf_op jit(solution)/shard_map/all_gather | solution.py:232
  1539.4 178.7 %copy-start.32 = (bf16[256,2048]{1,0:T(8,128)(2,1)S(1)}, bf16[256,2048]{1,0:T(8,128)(2,1)}, u32[]{:S(2)}) copy-start(bf16[256,2048]{1,0:T(8,128)(2,1)} %param.22) | copy-start | bytes 3145732
  1542.5 309.3 %all-gather.22.cloned.1.call-start = ((), (), s32[]{:S(2)}) async-start(), calls=%async_computation.27 | async-start | bytes 2096640 | tf_op jit(solution)/shard_map/all_gather | solution.py:17
  1727.6 48.3 %copy-start.12 = (bf16[1024,3,2,128]{0,3,2,1:T(8,128)(2,1)}, bf16[1024,3,2,128]{0,3,2,1:T(8,128)(2,1)S(1)}, u32[]{:S(2)}) copy-start(bf16[1024,3,2,128]{0,3,2,1:T(8,128)(2,1)S(1)} %divide_convert_fusion) | copy-start | bytes 4718596
  1732.1 190.3 %reduce-scatter.32.cloned.1.call-start = ((), (), s32[]{:S(2)}) async-start(), calls=%async_computation.25 | async-start | bytes 3522560 | tf_op jit(solution)/shard_map/reduce_scatter | solution.py:354
  1746.6 178.1 %reduce-scatter.30.cloned.1.call-start = ((), (), s32[]{:S(2)}) async-start(), calls=%async_computation.24 | async-start | bytes 3522560 | tf_op jit(solution)/shard_map/reduce_scatter | solution.py:351
  1761.0 166.1 %reduce-scatter.28.cloned.1.call-start = ((), (), s32[]{:S(2)}) async-start(), calls=%async_computation.23 | async-start | bytes 3522560 | tf_op jit(solution)/shard_map/reduce_scatter | solution.py:348
  1761.1 14.8 copy-start.36
  1761.1 14.8 copy-start.51
  1761.1 14.8 copy-start.53
  1761.1 14.8 copy-start.7
  1761.1 14.8 copy-start.43
  1775.8 153.7 %reduce-scatter.20.cloned.1.call-start = ((), (), s32[]{:S(2)}) async-start(), calls=%async_computation.19 | async-start | bytes 163840 | tf_op jit(solution)/shard_map/reduce_scatter | solution.py:336
  1780.0 27.6 %slice-start = ((s8[12582912]{0:T(1024)(128)(4,1)}), s8[4194304]{0:T(1024)(128)(4,1)S(1)}, s32[]{:S(2)}) async-start(s8[12582912]{0:T(1024)(128)(4,1)} %bitcast.219), calls=%async_computation.28 | async-start | bytes 8388608
  1783.6 17.5 copy-start.28
  1783.6 24.0 %slice-start.1 = ((s8[12582912]{0:T(1024)(128)(4,1)}), s8[4194304]{0:T(1024)(128)(4,1)S(1)}, s32[]{:S(2)}) async-start(s8[12582912]{0:T(1024)(128)(4,1)} %bitcast.219), calls=%async_computation.29 | async-start | bytes 8388608
  1783.6 24.0 %slice-start.2 = ((s8[12582912]{0:T(1024)(128)(4,1)}), s8[4194304]{0:T(1024)(128)(4,1)S(1)}, s32[]{:S(2)}) async-start(s8[12582912]{0:T(1024)(128)(4,1)} %bitcast.219), calls=%async_computation.30 | async-start | bytes 8388608
  1831.5 99.5 %reduce-scatter.26.cloned.1.call-start = ((), (), s32[]{:S(2)}) async-start(), calls=%async_computation.22 | async-start | bytes 1310720 | tf_op jit(solution)/shard_map/reduce_scatter | solution.py:345
  1851.7 86.6 %reduce-scatter.22.cloned.1.call-start = ((), (), s32[]{:S(2)}) async-start(), calls=%async_computation.20 | async-start | bytes 163840 | tf_op jit(solution)/shard_map/reduce_scatter | solution.py:339
  1892.1 74.1 %reduce-scatter.24.cloned.1.call-start = ((), (), s32[]{:S(2)}) async-start(), calls=%async_computation.21 | async-start | bytes 1310720 | tf_op jit(solution)/shard_map/reduce_scatter | solution.py:342
  1900.1 277.7 %reduce-scatter.18.cloned.1.call-start = ((), (), s32[]{:S(2)}) async-start(), calls=%async_computation.18 | async-start | bytes 14155776 | tf_op jit(solution)/shard_map/reduce_scatter | solution.py:311
  1922.3 255.5 %copy-start.55 = (f32[2048]{0:T(1024)S(1)}, f32[2048]{0:T(1024)}, u32[]{:S(2)}) copy-start(f32[2048]{0:T(1024)} %param.18) | copy-start | bytes 24580
  1922.3 255.5 %copy-start.59 = (f32[128,3]{0,1:T(4,128)S(1)}, f32[128,3]{0,1:T(4,128)}, u32[]{:S(2)}) copy-start(f32[128,3]{0,1:T(4,128)} %copy-done.58) | copy-start | bytes 4612
  1924.7 256.2 %copy-start.56 = (f32[2048]{0:T(1024)S(1)}, f32[2048]{0:T(1024)}, u32[]{:S(2)}) copy-start(f32[2048]{0:T(1024)} %get-tuple-element.230) | copy-start | bytes 24580
  1924.7 256.2 %copy-start.57 = (f32[2048]{0:T(1024)S(1)}, f32[2048]{0:T(1024)}, u32[]{:S(2)}) copy-start(f32[2048]{0:T(1024)} %get-tuple-element.271) | copy-start | bytes 24580
  2177.8 49.5 %copy-start.1 = (bf16[688,2048]{1,0:T(8,128)(2,1)S(1)}, bf16[688,2048]{1,0:T(8,128)(2,1)}, u32[]{:S(2)}) copy-start(bf16[688,2048]{1,0:T(8,128)(2,1)} %param.27) | copy-start | bytes 8454148
  (45 other events, 235.8 us)
Sparse Core Ops, SparseCore 0:
  12.9 179.1 all-gather.11
  230.1 18.4 all-gather.19
  287.7 412.2 reduce-scatter.11
  706.3 175.5 all-gather.13
  883.9 174.6 all-gather.15
  1116.9 205.9 reduce-scatter.15
  1326.6 206.8 reduce-scatter.13
  1542.6 175.5 all-gather.17
  1732.2 18.4 all-gather.21
  1753.1 35.9 reduce-scatter.31
  1791.8 35.9 reduce-scatter.29
  1830.2 36.0 reduce-scatter.27
  1869.4 19.5 reduce-scatter.19
  1891.4 24.8 reduce-scatter.25
  1918.7 19.5 reduce-scatter.21
  1941.3 24.8 reduce-scatter.23
  1970.1 207.6 reduce-scatter.17
where the time goes:
time: 2240 us; the launch traced here: 2230 us
  waiting for transfers between devices  1720 us (77%)
  matrix products  349 us (16%)
  other arithmetic  66.9 us (3%)
  blocking collectives  58.4 us (3%)
  local copies, waits for them, and re-layouts  25.8 us (1%)
    reduce_scatter x1, waiting for transfers between devices, on_device(): lax.psum_scatter(jnp.einsum('trc,cd->trd', row_segment, w_out, preferred_...  412 us
    reduce_scatter x1, waiting for transfers between devices, on_device(): lax.psum_scatter((summed + jnp.einsum('trc,dc->trd', grad_value_low, w_va...  210 us
    reduce_scatter x1, waiting for transfers between devices, on_device(): lax.psum_scatter(jnp.einsum('nzh,hi->nzi', row_segment, down_weight, pref...  206 us
    reduce_scatter x1, waiting for transfers between devices, on_device(): lax.psum_scatter((jnp.einsum('szq,hq->szh', gate_gradient, gate_weight, p...  191 us
    all_gather x1, waiting for transfers between devices, on_device(): lax.all_gather(grad_middle.astype(jnp.bfloat16), 'head', axis=0, tiled=True)  176 us
    all_gather x1, waiting for transfers between devices, on_device(): lax.all_gather(normed_two_low, 'head', axis=0, tiled=True)  175 us
    all_gather x1, waiting for transfers between devices, on_device(): normed_full = lax.all_gather(normed_low, 'head', axis=0, tiled=True)  164 us
    all_gather x1, waiting for transfers between devices, on_device(): lax.all_gather(cotangent, 'head', axis=0, tiled=True)  150 us
  transfers between devices with their start and end apart: 17, of which 10 were waited for; matrix products, arithmetic and copies ran while one was open for 12% of the time, Pallas kernels for 0%

commit v1 on v0

--- a/solution.py
+++ b/solution.py
@@ -7,6 +7,16 @@
 epsilon = 1e-05
 root_half = 0.7071067811865476
 exact_precision_flag = lax.Precision.HIGHEST
+
+
+def gather_by_hops(x, axis, dim):
+    size = lax.axis_size(axis)
+    moving, parts = (x, [x])
+    for _ in range(size - 1):
+        moving = lax.ppermute(moving, axis, [(i, (i + 1) % size) for i in range(size)])
+        parts.insert(0, moving)
+    line = jnp.concatenate(parts, axis=dim)
+    return jnp.roll(line, (lax.axis_index(axis) + 1) * x.shape[dim], axis=dim)
 
 
 def entering(array, axis, join, neutral, backward):
@@ -92,7 +102,7 @@
     scale_one = rms_scale(x_float)
     normed_one = x_float * scale_one
     normed_low = (normed_one * attn_gain).astype(jnp.bfloat16)
-    normed_full = lax.all_gather(normed_low, "head", axis=0, tiled=True)
+    normed_full = gather_by_hops(normed_low, "head", 0)
     query_low = (
         jnp.einsum("trd,dc->trc", normed_full, w_query, preferred_element_type=jnp.float32)
         .astype(jnp.bfloat16)

time: 2240 us -> 2330 us (1.040)
  waiting for transfers between devices: 1720 us -> 1790 us
    ppermute x0 -> x7, waiting for transfers between devices: none -> 241 us  [gather_by_hops(): lax.ppermute(moving, axis, [(i, (i + 1) % size) for i in range(size)])]
    all_gather x1 -> x0, waiting for transfers between devices: 164 us -> none  [on_device(): normed_full = lax.all_gather(normed_low, 'head', axis=0, tiled=True)]
  transfers between devices with their start and end apart: 17 -> 23, of which waited for: 10 -> 16; matrix products, arithmetic and copies ran while one was open for 12% -> 12% of each run, Pallas kernels for 0% -> 0%
where the time goes in v1:
time: 2330 us; the launch traced here: 2320 us
  waiting for transfers between devices  1790 us (77%)
  matrix products  352 us (15%)
  other arithmetic  67.7 us (3%)
  blocking collectives  55.9 us (2%)
  local copies, waits for them, and re-layouts  38.2 us (2%)
    reduce_scatter x1, waiting for transfers between devices, on_device(): lax.psum_scatter(jnp.einsum('trc,cd->trd', row_segment, w_out, preferred_...  410 us
    ppermute x7, waiting for transfers between devices, gather_by_hops(): lax.ppermute(moving, axis, [(i, (i + 1) % size) for i in range(size)])  241 us
    reduce_scatter x1, waiting for transfers between devices, on_device(): lax.psum_scatter((summed + jnp.einsum('trc,dc->trd', grad_value_low, w_va...  210 us
    reduce_scatter x1, waiting for transfers between devices, on_device(): lax.psum_scatter(jnp.einsum('nzh,hi->nzi', row_segment, down_weight, pref...  206 us
    reduce_scatter x1, waiting for transfers between devices, on_device(): lax.psum_scatter((jnp.einsum('szq,hq->szh', gate_gradient, gate_weight, p...  191 us
    all_gather x1, waiting for transfers between devices, on_device(): lax.all_gather(grad_middle.astype(jnp.bfloat16), 'head', axis=0, tiled=True)  176 us
    all_gather x1, waiting for transfers between devices, on_device(): lax.all_gather(normed_two_low, 'head', axis=0, tiled=True)  175 us
    all_gather x1, waiting for transfers between devices, on_device(): lax.all_gather(cotangent, 'head', axis=0, tiled=True)  150 us
  transfers between devices with their start and end apart: 23, of which 16 were waited for; matrix products, arithmetic and copies ran while one was open for 12% of the time, Pallas kernels for 0%

profile of v1, /device:TPU:0, one launch (start us, length us, event | category | flops | bytes accessed | tf_op | source)
XLA Modules:
  0.0 2321.1 jit_solution(12737461303045252977)
XLA Ops:
  14.1 37.4 %collective-permute-done = bf16[128,3,2048]{2,0,1:T(8,128)(2,1)S(1)} collective-permute-done((bf16[128,3,2048]{2,0,1:T(8,128)(2,1)S(1)}, bf16[128,3,2048]{2,0,1:T(8,128)(2,1)S(1)}, u32[]{:S(2)}, u32[]{:S(2)}) %collective-permute-start) | collective-permute-done | bytes 1572896 | tf_op jit(solution)/shard_map/ppermute | solution.py:16
  52.6 38.3 %collective-permute-done.1 = bf16[128,3,2048]{2,0,1:T(8,128)(2,1)S(1)} collective-permute-done((bf16[128,3,2048]{2,0,1:T(8,128)(2,1)S(1)}, bf16[128,3,2048]{2,0,1:T(8,128)(2,1)S(1)}, u32[]{:S(2)}, u32[]{:S(2)}) %collective-permute-start.1) | collective-permute-done | bytes 1572896 | tf_op jit(solution)/shard_map/ppermute | solution.py:16
  92.1 37.4 %collective-permute-done.2 = bf16[128,3,2048]{2,0,1:T(8,128)(2,1)S(1)} collective-permute-done((bf16[128,3,2048]{2,0,1:T(8,128)(2,1)S(1)}, bf16[128,3,2048]{2,0,1:T(8,128)(2,1)S(1)}, u32[]{:S(2)}, u32[]{:S(2)}) %collective-permute-start.2) | collective-permute-done | bytes 1572896 | tf_op jit(solution)/shard_map/ppermute | solution.py:16
  130.6 36.4 %collective-permute-done.3 = bf16[128,3,2048]{2,0,1:T(8,128)(2,1)S(1)} collective-permute-done((bf16[128,3,2048]{2,0,1:T(8,128)(2,1)S(1)}, bf16[128,3,2048]{2,0,1:T(8,128)(2,1)S(1)}, u32[]{:S(2)}, u32[]{:S(2)}) %collective-permute-start.3) | collective-permute-done | bytes 1572896 | tf_op jit(solution)/shard_map/ppermute | solution.py:16
  168.2 35.6 %collective-permute-done.4 = bf16[128,3,2048]{2,0,1:T(8,128)(2,1)} collective-permute-done((bf16[128,3,2048]{2,0,1:T(8,128)(2,1)S(1)}, bf16[128,3,2048]{2,0,1:T(8,128)(2,1)}, u32[]{:S(2)}, u32[]{:S(2)}) %collective-permute-start.4) | collective-permute-done | bytes 1572896 | tf_op jit(solution)/shard_map/ppermute | solution.py:16
  203.8 34.9 %collective-permute-done.5 = bf16[128,3,2048]{2,0,1:T(8,128)(2,1)} collective-permute-done((bf16[128,3,2048]{2,0,1:T(8,128)(2,1)}, bf16[128,3,2048]{2,0,1:T(8,128)(2,1)}, u32[]{:S(2)}, u32[]{:S(2)}) %collective-permute-start.5) | collective-permute-done | bytes 1572896 | tf_op jit(solution)/shard_map/ppermute | solution.py:16
  240.7 5.8 all-reduce
  251.2 21.4 collective-permute-done.6
  296.4 14.3 fusion.70
  324.5 5.2 all-gather.2
  329.8 16.6 convert_reduce_fusion
  346.4 8.0 fusion.139
  366.7 10.1 fusion.97
  376.9 410.0 %reduce-scatter.12.cloned.1.call-done = f32[128,3,2048]{2,0,1:T(8,128)} async-done(((f32[1024,3,2048]{2,0,1:T(8,128)}), f32[128,3,2048]{2,0,1:T(8,128)}) %reduce-scatter.12.cloned.1.call-update) | async-done | bytes 3145744 | tf_op jit(solution)/shard_map/reduce_scatter | solution.py:165
  793.6 175.1 %all-gather.11.cloned.1.call-done = bf16[1024,3,2048]{2,0,1:T(8,128)(2,1)} async-done(((bf16[128,3,2048]{2,0,1:T(8,128)(2,1)}), bf16[1024,3,2048]{2,0,1:T(8,128)(2,1)}) %all-gather.11.cloned.1.call-update) | async-done | bytes 12582928 | tf_op jit(solution)/shard_map/all_gather | solution.py:186
  968.7 15.2 fusion.45
  983.9 11.3 fusion.49
  995.1 150.2 %all-gather.13.cloned.1.call-done = bf16[1024,3,2048]{2,0,1:T(8,128)(2,1)} async-done(((bf16[128,3,2048]{2,0,1:T(8,128)(2,1)}), bf16[1024,3,2048]{2,0,1:T(8,128)(2,1)}) %all-gather.13.cloned.1.call-update) | async-done | bytes 12582928 | tf_op jit(solution)/shard_map/all_gather | solution.py:201
  1145.4 22.1 multiply_convert_fusion
  1167.5 17.4 fusion.47
  1184.9 18.9 add_convert_fusion.1
  1203.8 15.0 convolution_convert_fusion
  1219.0 190.8 %reduce-scatter.16.cloned.1.call-done = bf16[128,3,2048]{2,0,1:T(8,128)(2,1)} async-done(((bf16[1024,3,2048]{2,0,1:T(8,128)(2,1)}), bf16[128,3,2048]{2,0,1:T(8,128)(2,1)}) %reduce-scatter.16.cloned.1.call-update) | async-done | bytes 1572880 | tf_op jit(solution)/shard_map/reduce_scatter | solution.py:224
  1413.8 206.4 %reduce-scatter.14.cloned.1.call-done = bf16[128,3,2048]{2,0,1:T(8,128)(2,1)} async-done(((bf16[1024,3,2048]{2,0,1:T(8,128)(2,1)}), bf16[128,3,2048]{2,0,1:T(8,128)(2,1)}) %reduce-scatter.14.cloned.1.call-update) | async-done | bytes 1572880 | tf_op jit(solution)/shard_map/reduce_scatter | solution.py:190
  1620.2 6.0 fusion.135
  1629.2 175.7 %all-gather.15.cloned.1.call-done = bf16[1024,3,2048]{2,0,1:T(8,128)(2,1)} async-done(((bf16[128,3,2048]{2,0,1:T(8,128)(2,1)}), bf16[1024,3,2048]{2,0,1:T(8,128)(2,1)}) %all-gather.15.cloned.1.call-update) | async-done | bytes 12582928 | tf_op jit(solution)/shard_map/all_gather | solution.py:242
  1804.9 9.0 multiply_reduce_fusion.5
  1818.8 14.4 bitcast_convert_fusion
  1833.3 14.3 bitcast_convert_fusion.1
  1847.7 14.8 bitcast_convert_fusion.2
  1868.3 16.5 select_convert_fusion
  1884.9 7.3 fusion.87
  1892.2 8.0 fusion.64
  1900.2 10.2 fusion.114
  1910.4 10.6 fusion.140
  1921.2 10.8 fusion.54
  1932.0 4.9 fusion.124
  1936.9 5.2 all-gather.4
  1942.3 4.9 while.31
  1954.4 8.1 fusion.88
  1964.4 7.5 fusion.67
  1971.9 11.5 fusion.99
  1983.6 8.0 fusion.55
  1991.7 22.2 add_convert_fusion
  2026.5 26.5 %reduce-scatter.24.cloned.1.call-done = bf16[512,256]{1,0:T(8,128)(2,1)} async-done(((bf16[2048,256]{1,0:T(8,128)(2,1)}), bf16[512,256]{1,0:T(8,128)(2,1)}) %reduce-scatter.24.cloned.1.call-update) | async-done | bytes 262160 | tf_op jit(solution)/shard_map/reduce_scatter | solution.py:352
  2054.8 209.9 %reduce-scatter.18.cloned.1.call-done = bf16[128,3,2048]{2,0,1:T(8,128)(2,1)} async-done(((bf16[1024,3,2048]{2,0,1:T(8,128)(2,1)}), bf16[128,3,2048]{2,0,1:T(8,128)(2,1)}) %reduce-scatter.18.cloned.1.call-update) | async-done | bytes 1572880 | tf_op jit(solution)/shard_map/reduce_scatter | solution.py:321
  2267.8 39.7 %all-reduce.4 = (f32[2048]{0:T(1024)S(1)}, f32[2048]{0:T(1024)S(1)}, f32[2048]{0:T(1024)S(1)}) all-reduce(f32[2048]{0:T(1024)S(1)} %get-tuple-element.232, f32[2048]{0:T(1024)S(1)} %copy-done.68, f32[2048]{0:T(1024)S(1)} %copy-done.67), channel_id=11, replica_groups=mesh['seq'=4,'head'=8] {'seq','head'}, use_global_device_ids=true, to_apply=%region_23.24.clone | all-reduce | flops 6144 | bytes 49152
  2309.2 4.9 fusion.28
  (298 shorter events, 125.4 us)
Async XLA Ops:
  7.2 1138.2 %copy-start = (bf16[688,2048]{1,0:T(8,128)(2,1)S(1)}, bf16[688,2048]{1,0:T(8,128)(2,1)}, u32[]{:S(2)}) copy-start(bf16[688,2048]{1,0:T(8,128)(2,1)} %param.27) | copy-start | bytes 8454148
  7.2 231.5 %copy-start.78 = (u32[32]{0:T(128)S(1)}, u32[32]{0:T(128)}, u32[]{:S(2)}) copy-start(u32[32]{0:T(128)} %constant.139) | copy-start | bytes 388
  7.2 232.7 %copy-start.70 = (s32[3,8]{1,0:T(4,128)S(1)}, s32[3,8]{1,0:T(4,128)}, u32[]{:S(2)}) copy-start(s32[3,8]{1,0:T(4,128)} %param.29) | copy-start | bytes 292
  7.2 347.2 %all-gather.17.cloned.1.call-start = ((), (), s32[]{:S(2)}) async-start(), calls=%async_computation.25 | async-start | bytes 2096640 | tf_op jit(solution)/shard_map/all_gather | solution.py:27
  9.2 276.0 %copy-start.65 = (f32[128,3]{0,1:T(4,128)}, f32[128,3]{0,1:T(4,128)S(1)}, u32[]{:S(2)}) copy-start(f32[128,3]{0,1:T(4,128)S(1)} %add_rsqrt_fusion.1) | copy-start | bytes 4612
  11.1 40.4 %collective-permute-start = (bf16[128,3,2048]{2,0,1:T(8,128)(2,1)S(1)}, bf16[128,3,2048]{2,0,1:T(8,128)(2,1)S(1)}, u32[]{:S(2)}, u32[]{:S(2)}) collective-permute-start(bf16[128,3,2048]{2,0,1:T(8,128)(2,1)S(1)} %fusion.33), channel_id=1, source_target_pairs={{0,1},{1,2},{2,3},{3,4},{4,5},{5,6},{6,7},{7,0},{8,9},{9,10},{10,1... | collective-permute-start | bytes 4718600 | tf_op jit(solution)/shard_map/ppermute | solution.py:16
  52.6 38.3 %collective-permute-start.1 = (bf16[128,3,2048]{2,0,1:T(8,128)(2,1)S(1)}, bf16[128,3,2048]{2,0,1:T(8,128)(2,1)S(1)}, u32[]{:S(2)}, u32[]{:S(2)}) collective-permute-start(bf16[128,3,2048]{2,0,1:T(8,128)(2,1)S(1)} %collective-permute-done), channel_id=1, source_target_pairs={{0,1},{1,2},{2,3},{3,4},{4,5},{5,6},{6,7},{7,0},{8,9},{9,10},{10,1... | collective-permute-start | bytes 4718600 | tf_op jit(solution)/shard_map/ppermute | solution.py:16
  92.1 37.4 %collective-permute-start.2 = (bf16[128,3,2048]{2,0,1:T(8,128)(2,1)S(1)}, bf16[128,3,2048]{2,0,1:T(8,128)(2,1)S(1)}, u32[]{:S(2)}, u32[]{:S(2)}) collective-permute-start(bf16[128,3,2048]{2,0,1:T(8,128)(2,1)S(1)} %collective-permute-done.1), channel_id=1, source_target_pairs={{0,1},{1,2},{2,3},{3,4},{4,5},{5,6},{6,7},{7,0},{8,9},{9,10},{10,1... | collective-permute-start | bytes 4718600 | tf_op jit(solution)/shard_map/ppermute | solution.py:16
  130.6 36.4 %collective-permute-start.3 = (bf16[128,3,2048]{2,0,1:T(8,128)(2,1)S(1)}, bf16[128,3,2048]{2,0,1:T(8,128)(2,1)S(1)}, u32[]{:S(2)}, u32[]{:S(2)}) collective-permute-start(bf16[128,3,2048]{2,0,1:T(8,128)(2,1)S(1)} %collective-permute-done.2), channel_id=1, source_target_pairs={{0,1},{1,2},{2,3},{3,4},{4,5},{5,6},{6,7},{7,0},{8,9},{9,10},{10,1... | collective-permute-start | bytes 4718600 | tf_op jit(solution)/shard_map/ppermute | solution.py:16
  168.2 35.6 %collective-permute-start.4 = (bf16[128,3,2048]{2,0,1:T(8,128)(2,1)S(1)}, bf16[128,3,2048]{2,0,1:T(8,128)(2,1)}, u32[]{:S(2)}, u32[]{:S(2)}) collective-permute-start(bf16[128,3,2048]{2,0,1:T(8,128)(2,1)S(1)} %collective-permute-done.3), channel_id=1, source_target_pairs={{0,1},{1,2},{2,3},{3,4},{4,5},{5,6},{6,7},{7,0},{8,9},{9,10},{10,1... | collective-permute-start | bytes 4718600 | tf_op jit(solution)/shard_map/ppermute | solution.py:16
  203.8 34.9 %collective-permute-start.5 = (bf16[128,3,2048]{2,0,1:T(8,128)(2,1)}, bf16[128,3,2048]{2,0,1:T(8,128)(2,1)}, u32[]{:S(2)}, u32[]{:S(2)}) collective-permute-start(bf16[128,3,2048]{2,0,1:T(8,128)(2,1)} %collective-permute-done.4), channel_id=1, source_target_pairs={{0,1},{1,2},{2,3},{3,4},{4,5},{5,6},{6,7},{7,0},{8,9},{9,10},{10,1... | collective-permute-start | bytes 4718600 | tf_op jit(solution)/shard_map/ppermute | solution.py:16
  238.7 34.0 %collective-permute-start.6 = (bf16[128,3,2048]{2,0,1:T(8,128)(2,1)}, bf16[128,3,2048]{2,0,1:T(8,128)(2,1)}, u32[]{:S(2)}, u32[]{:S(2)}) collective-permute-start(bf16[128,3,2048]{2,0,1:T(8,128)(2,1)} %collective-permute-done.5), channel_id=1, source_target_pairs={{0,1},{1,2},{2,3},{3,4},{4,5},{5,6},{6,7},{7,0},{8,9},{9,10},{10,1... | collective-permute-start | bytes 4718600 | tf_op jit(solution)/shard_map/ppermute | solution.py:16
  246.6 114.3 %copy-start.72 = (bf16[273]{0:T(512)(128)(2,1)}, bf16[273]{0:T(512)(128)(2,1)S(1)}, u32[]{:S(2)}) copy-start(bf16[273]{0:T(512)(128)(2,1)S(1)} %pad.3.clone) | copy-start | bytes 1642
  247.7 73.1 %copy-start.52 = (f32[1024,3]{0,1:T(4,128)}, f32[1024,3]{0,1:T(4,128)S(1)}, u32[]{:S(2)}) copy-start(f32[1024,3]{0,1:T(4,128)S(1)} %get-tuple-element.297) | copy-start | bytes 36868
  247.7 113.2 %copy-start.41 = (f32[3,1024]{1,0:T(4,128)}, f32[3,1024]{1,0:T(4,128)S(1)}, u32[]{:S(2)}) copy-start(f32[3,1024]{1,0:T(4,128)S(1)} %get-tuple-element.276) | copy-start | bytes 36868
  251.2 26.4 %copy-start.25 = (bf16[128,3,2048]{2,0,1:T(8,128)(2,1)S(1)}, bf16[128,3,2048]{2,0,1:T(8,128)(2,1)}, u32[]{:S(2)}) copy-start(bf16[128,3,2048]{2,0,1:T(8,128)(2,1)} %copy-done.24) | copy-start | bytes 4718596
  289.8 40.0 %copy-start.31 = (bf16[1024,3,32]{0,2,1:T(8,128)(2,1)}, bf16[1024,3,32]{0,2,1:T(8,128)(2,1)S(1)}, u32[]{:S(2)}) copy-start(bf16[1024,3,32]{0,2,1:T(8,128)(2,1)S(1)} %fusion.89) | copy-start | bytes 589828
  294.7 16.0 copy-start.33
  295.4 21.7 copy-start.15
  320.7 466.2 %reduce-scatter.12.cloned.1.call-start = ((), (), s32[]{:S(2)}) async-start(), calls=%async_computation.11 | async-start | bytes 28311552 | tf_op jit(solution)/shard_map/reduce_scatter | solution.py:165
  329.8 16.6 copy-start.8
  376.8 410.1 %copy-start.69 = (f32[2048]{0:T(1024)S(1)}, f32[2048]{0:T(1024)}, u32[]{:S(2)}) copy-start(f32[2048]{0:T(1024)} %param.23) | copy-start | bytes 24580
  376.8 414.7 %copy-start.64 = (f32[2048]{0:T(1024)S(1)}, f32[2048]{0:T(1024)}, u32[]{:S(2)}) copy-start(f32[2048]{0:T(1024)} %param.24) | copy-start | bytes 24580
  376.9 591.8 %all-gather.11.cloned.1.call-start = ((), (), s32[]{:S(2)}) async-start(), calls=%async_computation.12 | async-start | bytes 14155776 | tf_op jit(solution)/shard_map/all_gather | solution.py:186
  793.0 352.4 %all-gather.13.cloned.1.call-start = ((), (), s32[]{:S(2)}) async-start(), calls=%async_computation.14 | async-start | bytes 14155776 | tf_op jit(solution)/shard_map/all_gather | solution.py:201
  793.6 616.2 %reduce-scatter.16.cloned.1.call-start = ((), (), s32[]{:S(2)}) async-start(), calls=%async_computation.15 | async-start | bytes 14155776 | tf_op jit(solution)/shard_map/reduce_scatter | solution.py:224
  968.7 15.2 copy-start.74
  968.7 15.2 copy-start.75
  1203.8 416.4 %reduce-scatter.14.cloned.1.call-start = ((), (), s32[]{:S(2)}) async-start(), calls=%async_computation.13 | async-start | bytes 14155776 | tf_op jit(solution)/shard_map/reduce_scatter | solution.py:190
  1218.9 401.3 %copy-start.26 = (bf16[128,3,2048]{2,0,1:T(8,128)(2,1)S(1)}, bf16[128,3,2048]{2,0,1:T(8,128)(2,1)}, u32[]{:S(2)}) copy-start(bf16[128,3,2048]{2,0,1:T(8,128)(2,1)} %param.28) | copy-start | bytes 4718596
  1218.9 586.0 %all-gather.15.cloned.1.call-start = ((), (), s32[]{:S(2)}) async-start(), calls=%async_computation.16 | async-start | bytes 14155776 | tf_op jit(solution)/shard_map/all_gather | solution.py:242
  1626.2 178.7 %copy-start.39 = (bf16[256,2048]{1,0:T(8,128)(2,1)S(1)}, bf16[256,2048]{1,0:T(8,128)(2,1)}, u32[]{:S(2)}) copy-start(bf16[256,2048]{1,0:T(8,128)(2,1)} %param.22) | copy-start | bytes 3145732
  1629.2 313.0 %all-gather.19.cloned.1.call-start = ((), (), s32[]{:S(2)}) async-start(), calls=%async_computation.26 | async-start | bytes 2096640 | tf_op jit(solution)/shard_map/all_gather | solution.py:27
  1814.4 48.3 %copy-start.10 = (bf16[1024,3,2,128]{0,3,2,1:T(8,128)(2,1)}, bf16[1024,3,2,128]{0,3,2,1:T(8,128)(2,1)S(1)}, u32[]{:S(2)}) copy-start(bf16[1024,3,2,128]{0,3,2,1:T(8,128)(2,1)S(1)} %divide_convert_fusion) | copy-start | bytes 4718596
  1818.8 195.2 %reduce-scatter.32.cloned.1.call-start = ((), (), s32[]{:S(2)}) async-start(), calls=%async_computation.24 | async-start | bytes 3522560 | tf_op jit(solution)/shard_map/reduce_scatter | solution.py:364
  1833.3 183.1 %reduce-scatter.30.cloned.1.call-start = ((), (), s32[]{:S(2)}) async-start(), calls=%async_computation.23 | async-start | bytes 3522560 | tf_op jit(solution)/shard_map/reduce_scatter | solution.py:361
  1847.6 171.2 %reduce-scatter.28.cloned.1.call-start = ((), (), s32[]{:S(2)}) async-start(), calls=%async_computation.22 | async-start | bytes 3522560 | tf_op jit(solution)/shard_map/reduce_scatter | solution.py:358
  1862.5 158.7 %reduce-scatter.20.cloned.1.call-start = ((), (), s32[]{:S(2)}) async-start(), calls=%async_computation.18 | async-start | bytes 163840 | tf_op jit(solution)/shard_map/reduce_scatter | solution.py:346
  1868.3 16.5 copy-start.35
  1921.0 101.6 %reduce-scatter.26.cloned.1.call-start = ((), (), s32[]{:S(2)}) async-start(), calls=%async_computation.21 | async-start | bytes 1310720 | tf_op jit(solution)/shard_map/reduce_scatter | solution.py:355
  1942.1 83.0 %reduce-scatter.22.cloned.1.call-start = ((), (), s32[]{:S(2)}) async-start(), calls=%async_computation.19 | async-start | bytes 163840 | tf_op jit(solution)/shard_map/reduce_scatter | solution.py:349
  1983.4 69.6 %reduce-scatter.24.cloned.1.call-start = ((), (), s32[]{:S(2)}) async-start(), calls=%async_computation.20 | async-start | bytes 1310720 | tf_op jit(solution)/shard_map/reduce_scatter | solution.py:352
  1991.6 273.0 %reduce-scatter.18.cloned.1.call-start = ((), (), s32[]{:S(2)}) async-start(), calls=%async_computation.17 | async-start | bytes 14155776 | tf_op jit(solution)/shard_map/reduce_scatter | solution.py:321
  2014.0 250.7 %copy-start.57 = (f32[2048]{0:T(1024)S(1)}, f32[2048]{0:T(1024)}, u32[]{:S(2)}) copy-start(f32[2048]{0:T(1024)} %param.18) | copy-start | bytes 24580
  2014.0 250.7 %copy-start.66 = (f32[128,3]{0,1:T(4,128)S(1)}, f32[128,3]{0,1:T(4,128)}, u32[]{:S(2)}) copy-start(f32[128,3]{0,1:T(4,128)} %copy-done.65) | copy-start | bytes 4612
  2016.4 251.4 %copy-start.67 = (f32[2048]{0:T(1024)S(1)}, f32[2048]{0:T(1024)}, u32[]{:S(2)}) copy-start(f32[2048]{0:T(1024)} %get-tuple-element.230) | copy-start | bytes 24580
  2016.4 251.4 %copy-start.68 = (f32[2048]{0:T(1024)S(1)}, f32[2048]{0:T(1024)}, u32[]{:S(2)}) copy-start(f32[2048]{0:T(1024)} %get-tuple-element.271) | copy-start | bytes 24580
  2264.6 49.6 %copy-start.1 = (bf16[688,2048]{1,0:T(8,128)(2,1)S(1)}, bf16[688,2048]{1,0:T(8,128)(2,1)}, u32[]{:S(2)}) copy-start(bf16[688,2048]{1,0:T(8,128)(2,1)} %param.27) | copy-start | bytes 8454148
  (54 other events, 301.3 us)
Sparse Core Ops, SparseCore 0:
  320.9 16.2 all-gather.16
  377.0 409.9 reduce-scatter.11
  793.1 175.5 all-gather.10
  970.7 174.6 all-gather.12
  1203.9 205.8 reduce-scatter.15
  1413.2 206.8 reduce-scatter.13
  1629.3 175.5 all-gather.14
  1818.9 18.4 all-gather.18
  1840.0 35.8 reduce-scatter.31
  1878.5 35.8 reduce-scatter.29
  1917.0 36.0 reduce-scatter.27
  1956.1 19.5 reduce-scatter.19
  1978.2 24.8 reduce-scatter.25
  2005.5 19.5 reduce-scatter.21
  2028.1 24.8 reduce-scatter.23
  2056.9 207.7 reduce-scatter.17
